TPU v7x, 256 devices: a whole 4x4x8 slice. The times are simulated.
256 devices in a mesh: depth: 2 (over core), row: 8 (over y_lo, x), col: 16 (over z, y_hi).
Axes of the slice: x: 4, y: 4 (y_hi: 2, y_lo: 2; y = y_hi * 2 + y_lo), z: 8, core: 2. Of those that a mesh axis runs over, the one named last changes fastest.
Arguments:
- a_blocks: float32 [64, 32, 4096], P('row', 'col'), may hold values from -0.75 to 0.75
- a_index: int32 [64, 32], P('row', 'col'), may hold values from -1 to 1023, as said below
- b_blocks: float32 [256, 16, 4096], P('col', 'row'), may hold values from -6 to 6
- b_index: int32 [256, 16], P('col', 'row'), may hold values from -1 to 1023, as said below
- c_index: int32 [64, 64], P('row', 'col'), may hold values from -1 to 15, as said below
Outputs:
- c_blocks: float32 [64, 64, 4096], P('row', 'col')
Inputs may be any that keep to these rules, and one draw needn't show every extreme that they name: `a_index`: slots j * 2 to (j + 1) * 2 - 1 of a block row hold block columns of k-panel j, that is j * 64 to (j + 1) * 64 - 1, or -1; the block columns of one row are distinct. Every slot group of some block rows is full. `b_index`: slots i * 2 to (i + 1) * 2 - 1 of a block column hold block rows i * 128 to (i + 1) * 128 - 1, or -1; the block rows of one column are distinct. Every slot group of some block columns is full. `c_index`: the kept block columns of one slot group of a row are distinct. Every slot group of some block rows is full.
All inputs are finite; a program needn't handle non-finite values.
Results may differ from a plain program's by a relative error of at most 0.0003.
Values sent between devices are 32-bit elements; how exact they have to be, the bound alone decides.
A program may use at most 128 MiB of HBM per device.

v0:
```python
import jax
import jax.numpy as jnp
from jax import lax
from jax.sharding import PartitionSpec as P

BS = 64
KB = 1024


def slot_lookup(indices, table_len):
    matches = indices[:, :, None] == jnp.arange(table_len, dtype=jnp.int32)[None, None, :]
    slot_ids = jnp.arange(indices.shape[1], dtype=jnp.int32)[None, :, None]
    located = jnp.any(matches, axis=1)
    return jnp.where(located, jnp.sum(jnp.where(matches, slot_ids, 0), axis=1), -1)


def per_device(a_blocks, a_index, b_blocks, b_index, c_index):
    rows_dev = a_index.shape[0]
    cols_dev = b_index.shape[0]
    layers = lax.axis_size("depth")
    layer_id = lax.axis_index("depth")
    c_share = c_index.shape[1] // layers
    c_sel = lax.dynamic_slice_in_dim(c_index, layer_id * c_share, c_share, 1)
    a_send, a_ids_send = (a_blocks, a_index)
    c_valid = c_sel >= 0
    c_safe = jnp.where(c_valid, c_sel, 0)
    empty = jnp.zeros((rows_dev, c_share, BS, BS), jnp.float32)
    b_whole, b_ids = (
        lax.all_gather(b_blocks, "row", axis=1, tiled=True),
        lax.all_gather(b_index, "row", axis=1, tiled=True),
    )
    b_table = slot_lookup(b_ids, KB)
    b_four = b_whole.reshape(cols_dev, b_ids.shape[1], BS, BS)
    a_part = lax.all_gather(a_send, "col", axis=1, tiled=True)
    a_ids = lax.all_gather(a_ids_send, "col", axis=1, tiled=True)
    slot_count = a_ids.shape[1]
    a_four = a_part.reshape(rows_dev, slot_count, BS, BS)
    k_safe = jnp.where(a_ids >= 0, a_ids, 0)
    u_ids = b_table[c_safe[:, :, None], k_safe[:, None, :]]
    usable = c_valid[:, :, None] & (a_ids >= 0)[:, None, :] & (u_ids >= 0)
    chosen = b_four[c_safe[:, :, None], jnp.where(usable, u_ids, 0)]
    chosen = jnp.where(usable[:, :, :, None, None], chosen, 0.0)
    totals = empty + jnp.einsum("rsac,rtscx->rtax", a_four, chosen, precision=lax.Precision.HIGHEST)
    flattened = totals.reshape(rows_dev, c_share, BS * BS)
    return lax.all_gather(flattened, "depth", axis=1, tiled=True)


def solution(mesh):
    placed = (
        P("row", "col", None),
        P("row", "col"),
        P("col", "row", None),
        P("col", "row"),
        P("row", "col"),
    )
    return jax.shard_map(
        per_device, mesh=mesh, in_specs=placed, out_specs=P("row", "col", None), check_vma=False
    )
```

profile of v0, /device:TPU:1, one launch (start us, length us, event | category | flops | bytes accessed | tf_op | source)
XLA Modules:
  0.0 215.6 jit_solution(7968068942080333352)
XLA Ops:
  6.5 0.0 all-gather.5.cloned.1.call-start
  6.5 2.1 copy.39
  8.7 0.0 all-gather.5.cloned.1.call-update
  8.7 0.0 all-gather.7.cloned.1.call-start
  8.8 1.8 copy.42
  10.6 0.0 all-gather.7.cloned.1.call-update
  10.6 0.7 fusion.17
  11.3 0.1 copy.38
  11.4 38.3 %all-gather = s32[16,2,8]{2,1,0:T(2,128)S(1)} all-gather(s32[1,2,8]{2,1,0:T(2,128)} %bitcast.41), channel_id=1, replica_groups=mesh['depth'=2,'row'=8,'col'=16] {'col'}, dimensions={0}, use_global_device_ids=true | all-gather | bytes 1088 | tf_op jit(solution)/shard_map/all_gather | solution.py:35
  49.7 0.1 copy.36
  49.8 0.1 broadcast_or_fusion
  49.9 0.1 reshape.60
  49.9 16.0 %all-gather.1 = s32[8,2,16]{2,1,0:T(2,128)S(1)} all-gather(s32[1,2,16]{2,1,0:T(2,128)} %bitcast.42), channel_id=1, replica_groups=mesh['depth'=2,'row'=8,'col'=16] {'row'}, dimensions={0}, use_global_device_ids=true | all-gather | bytes 1152 | tf_op jit(solution)/shard_map/all_gather | solution.py:30
  66.0 0.1 copy.37
  66.0 0.3 fusion.10
  66.3 0.4 select_reduce_fusion
  66.7 4.5 %gather_fusion = s32[512]{0:T(512)S(1)} fusion(s32[16,1024]{1,0:T(8,128)S(1)} %broadcast_select_fusion, s32[512]{0:T(512)S(1)} %reshape.60), kind=kCustom, calls=%fused_computation | custom fusion | bytes 8192 | tf_op jit(solution)/shard_map/gather | solution.py:39
  71.3 0.1 gather.9
  71.3 0.1 copy.35
  71.4 0.1 fusion.13
  71.5 0.1 reshape.66
  71.6 0.1 reshape.74
  71.7 0.1 and_and_fusion
  71.8 0.0 all-gather.5.cloned.1.call-done
  71.8 7.9 %reshape.57 = f32[16,16,64,64]{3,2,0,1:T(8,128)} reshape(f32[16,16,4096]{2,0,1:T(8,128)} %all-gather.5.cloned.1.call-done) | data formatting | bytes 8388608 | tf_op jit(solution)/shard_map/reshape | solution.py:33
  79.7 13.4 %gather_fusion.1 = f32[512,64,64]{2,1,0:T(8,128)} fusion(f32[16,16,64,64]{3,2,0,1:T(8,128)} %reshape.57, s32[512]{0:T(512)S(1)} %reshape.66), kind=kCustom, calls=%fused_computation.1 | custom fusion | bytes 16781312 | tf_op jit(solution)/shard_map/gather | solution.py:41
  93.1 17.7 %copy.41 = f32[512,64,64]{1,2,0:T(8,128)} copy(f32[512,64,64]{2,1,0:T(8,128)} %gather_fusion.1) | data formatting | bytes 16777216 | tf_op jit(solution)/shard_map/gather | solution.py:41
  110.8 55.6 %all-gather.7.cloned.1.call-done = f32[8,32,4096]{2,0,1:T(8,128)} async-done(((f32[8,2,4096]{2,0,1:T(8,128)}), f32[8,32,4096]{2,0,1:T(8,128)}) %all-gather.7.cloned.1.call-update) | async-done | bytes 4194320 | tf_op jit(solution)/shard_map/all_gather | solution.py:34
  166.4 6.6 %copy.43 = f32[8,32,4096]{2,1,0:T(8,128)} copy(f32[8,32,4096]{2,0,1:T(8,128)} %all-gather.7.cloned.1.call-done) | data formatting | bytes 8388608 | tf_op jit(solution)/shard_map/all_gather | solution.py:34
  173.0 7.9 %reshape.79 = f32[8,32,64,64,1]{3,2,1,0,4:T(8,128)} reshape(f32[8,32,4096]{2,1,0:T(8,128)} %copy.43) | data formatting | bytes 8388608 | tf_op jit(solution)/shard_map/reshape | solution.py:37
  180.9 20.6 %fusion.5 = f32[8,2,64,64]{2,3,1,0:T(8,128)S(1)} fusion(f32[8,32,64,64,1]{3,2,1,0,4:T(8,128)} %reshape.79, f32[8,2,32,64,64]{3,4,2,1,0:T(8,128)} %bitcast.38, pred[8,2,32]{2,1,0:T(4,128)(4,1)S(1)} %and_and_fusion), kind=kOutput, calls=%fused_computation.7 | convolution fusion | flops 1612709888 | bytes 12845568 | tf_op jit(solution)/shard_map/rsac,rtscx->rtax/dot_general | solution.py:43
  201.5 0.2 copy.44
  201.7 0.2 reshape.59
  201.9 5.7 %all_gather.19 = f32[8,4,4096]{2,0,1:T(8,128)S(1)} all-gather(f32[8,2,4096]{2,0,1:T(8,128)S(1)} %reshape.59), channel_id=1, replica_groups=mesh['depth'=2,'row'=8,'col'=16] {'depth'}, dimensions={1}, use_global_device_ids=true | all-gather | bytes 786432 | tf_op jit(solution)/shard_map/all_gather | solution.py:45
  207.6 1.1 copy.45
  (4 shorter events, 0.0 us)
Async XLA Ops:
  6.5 65.3 %all-gather.5.cloned.1.call-start = ((), (), s32[]{:S(2)}) async-start(), calls=%async_computation | async-start | bytes 4718592 | tf_op jit(solution)/shard_map/all_gather | solution.py:29
  8.7 157.7 %all-gather.7.cloned.1.call-start = ((), (), s32[]{:S(2)}) async-start(), calls=%async_computation.1 | async-start | bytes 4456448 | tf_op jit(solution)/shard_map/all_gather | solution.py:34
Sparse Core Ops, SparseCore 0:
  9.1 59.1 all-gather.4
  70.9 95.5 all-gather.6
where the time goes:
time: 217 us; the launch traced here: 216 us
  local copies, waits for them, and re-layouts  64.1 us (30%)
  blocking collectives  60.1 us (28%)
  waiting for transfers between devices  55.7 us (26%)
  matrix products  20.6 us (9%)
  between operations  13.5 us (6%)
    all_gather x1, waiting for transfers between devices, per_device(): a_part = lax.all_gather(a_send, 'col', axis=1, tiled=True)  55.6 us
    all_gather x1, blocking collectives, per_device(): a_ids = lax.all_gather(a_ids_send, 'col', axis=1, tiled=True)  38.3 us
    gather x2, local copies, waits for them, and re-layouts, per_device(): chosen = b_four[c_safe[:, :, None], jnp.where(usable, u_ids, 0)]  31.1 us
    dot_general x1, matrix products, per_device(): jnp.einsum('rsac,rtscx->rtax', a_four, chosen, precision=lax.Precision.HI...  20.6 us
    all_gather x1, blocking collectives, per_device(): lax.all_gather(b_index, 'row', axis=1, tiled=True)  16 us
    reshape x1, local copies, waits for them, and re-layouts, per_device(): b_four = b_whole.reshape(cols_dev, b_ids.shape[1], BS, BS)  7.87 us
    reshape x1, local copies, waits for them, and re-layouts, per_device(): a_four = a_part.reshape(rows_dev, slot_count, BS, BS)  7.86 us
    all_gather x1, local copies, waits for them, and re-layouts, per_device(): a_part = lax.all_gather(a_send, 'col', axis=1, tiled=True)  6.57 us
  transfers between devices with their start and end apart: 2, of which 1 were waited for; matrix products, arithmetic and copies ran while one was open for 22% of the time, Pallas kernels for 0%

commit v1 on v0

v1 whole, which is shorter than its diff:
```python
import jax
import jax.numpy as jnp
from jax import lax
from jax.experimental import pallas as pl
from jax.experimental.pallas import tpu as pltpu
from jax.sharding import PartitionSpec as P

BS = 64
LANES = 128
ROWS = 8
COLS = 16
A_DATA = ROWS * BS
A_CHUNK = A_DATA + ROWS * 2
B_DATA = COLS * 4
B_CHUNK = B_DATA + 1
A_HALF = A_CHUNK // 2
B_PARTS = ((0, B_DATA // 2 + 1), (B_DATA // 2 + 1, B_DATA // 2))
X, Z = 4, 8
MESH = pl.DeviceIdType.MESH


def halves(x0, x1, left):
    return (
        jnp.where(left, x0, pltpu.roll(x1, BS, 1)),
        jnp.where(left, pltpu.roll(x0, BS, 1), x1),
    )


def kernel(
    a_ref, ai_ref, b_ref, bi_ref, ci_ref, o_ref,
    abuf, bbuf, pbuf, rbuf,
    asend, arecv, bsend, brecv, csend, crecv,
):
    d = lax.axis_index("depth")
    row = lax.axis_index("row")
    col = lax.axis_index("col")
    x, yl = row % X, row // X
    z, yh = col // 2, col % 2

    def at_z(step):
        return {"depth": d, "row": row, "col": ((z + step + Z) % Z) * 2 + yh}

    def at_x(step):
        return {"depth": d, "row": yl * X + (x + step + X) % X, "col": col}

    yh_peer = {"depth": d, "row": row, "col": z * 2 + (1 - yh)}
    yl_peer = {"depth": d, "row": (1 - yl) * X + x, "col": col}
    core_peer = {"depth": 1 - d, "row": row, "col": col}

    barrier = pltpu.get_barrier_semaphore()
    for peer in (at_z(1), at_z(-1), at_x(1), at_x(-1), yh_peer, yl_peer, core_peer):
        pl.semaphore_signal(barrier, inc=1, device_id=peer, device_id_type=MESH)

    a_even = (z + d) % 2 == 0
    b_even = (x + d) % 2 == 0
    left = lax.broadcasted_iota(jnp.int32, (1, LANES), 1) < BS

    def a_slot(step):
        return ((z + step + Z) % Z) // 2

    def b_slot(step):
        return ((x + step + X) % X) // 2

    @pl.when(a_even)
    def _():
        slot = a_slot(0)
        for m in range(ROWS):
            x0 = a_ref[pl.ds(m * BS, 32, stride=2), :]
            x1 = a_ref[pl.ds(m * BS + 1, 32, stride=2), :]
            low, high = halves(x0, x1, left)
            abuf[slot, yh, pl.ds(m * BS, 32), :] = low
            abuf[slot, yh, pl.ds(m * BS + 32, 32), :] = high
            for s in range(2):
                v = jnp.full((1, LANES), ai_ref[m, s])
                v = jnp.where(v < 0, -1, v + 1).astype(jnp.float32)
                abuf[slot, yh, pl.ds(A_DATA + m * 2 + s, 1), :] = v

    @pl.when(b_even)
    def _():
        slot = b_slot(0)
        for n in range(COLS):
            x0 = b_ref[pl.ds(n * BS, 32, stride=2), :]
            x1 = b_ref[pl.ds(n * BS + 1, 32, stride=2), :]
            low, high = halves(x0, x1, left)
            for g in range(4):
                bbuf[yl, slot, n * 4 + g, pl.ds(0, 8, stride=2), :] = low[g * 8 : g * 8 + 8]
                bbuf[yl, slot, n * 4 + g, pl.ds(1, 8, stride=2), :] = high[g * 8 : g * 8 + 8]
            v0 = jnp.full((1, LANES), bi_ref[n, 0])
            v1 = jnp.full((1, LANES), bi_ref[n, 1])
            v = (jnp.where(left, v0, v1) + 1).astype(jnp.float32)
            bbuf[yl, slot, B_DATA, n : n + 1, :] = v

    pl.semaphore_wait(barrier, 7)

    def a_copy(slot, sub, to, nth, part=None):
        view = abuf.at[slot, sub]
        if part is not None:
            view = abuf.at[slot, sub, pl.ds(part * A_HALF, A_HALF), :]
        return pltpu.make_async_remote_copy(
            src_ref=view, dst_ref=view,
            send_sem=asend.at[nth], recv_sem=arecv.at[slot, sub, part or 0],
            device_id=to, device_id_type=MESH,
        )

    def b_copy(slot, sub, to, nth, part=None):
        view = bbuf.at[sub, slot]
        if part is not None:
            view = bbuf.at[sub, slot, pl.ds(*B_PARTS[part])]
        return pltpu.make_async_remote_copy(
            src_ref=view, dst_ref=view,
            send_sem=bsend.at[nth], recv_sem=brecv.at[sub, slot, part or 0],
            device_id=to, device_id_type=MESH,
        )

    def a_arrived(step, sub, part=None):
        a_copy(a_slot(step), sub, at_z(1), 0, part).wait_recv()

    def b_arrived(step, sub, part=None):
        b_copy(b_slot(step), sub, at_x(1), 0, part).wait_recv()

    mine, other = yh, 1 - yh
    bmine, bother = yl, 1 - yl
    a_own = [
        a_copy(a_slot(0), mine, yh_peer, 0),
        a_copy(a_slot(0), mine, at_z(1), 1),
        a_copy(a_slot(0), mine, at_z(-1), 2),
    ]
    a_swapped = [a_copy(a_slot(0), other, at_z(1), 3), a_copy(a_slot(0), other, at_z(-1), 4)]
    even = [
        [a_copy(a_slot(-2), s, at_z(1), 5 + 2 * i), a_copy(a_slot(2), s, at_z(-1), 6 + 2 * i)]
        for i, s in enumerate((mine, other))
    ]
    odd = [
        [a_copy(a_slot(-1), s, at_z(1), 2 * i), a_copy(a_slot(1), s, at_z(-1), 1 + 2 * i)]
        for i, s in enumerate((mine, other))
    ]
    odd_far = [
        [a_copy(a_slot(-3), s, at_z(1), 4 + 2 * i, 0), a_copy(a_slot(3), s, at_z(-1), 5 + 2 * i, 1)]
        for i, s in enumerate((mine, other))
    ]
    b_own = [
        b_copy(b_slot(0), bmine, yl_peer, 0),
        b_copy(b_slot(0), bmine, at_x(1), 1),
        b_copy(b_slot(0), bmine, at_x(-1), 2),
    ]
    b_swapped = [b_copy(b_slot(0), bother, at_x(1), 3), b_copy(b_slot(0), bother, at_x(-1), 4)]
    b_far = [
        [b_copy(b_slot(-1), s, at_x(1), 2 * i, 0), b_copy(b_slot(1), s, at_x(-1), 1 + 2 * i, 1)]
        for i, s in enumerate((bmine, bother))
    ]

    def start(copies):
        for c in copies:
            c.start()

    def forward(arrived, distance, sub, copies):
        for step, c in zip((-distance, distance), copies):
            arrived(step, sub)
            c.start()

    @pl.when(a_even)
    def _():
        start(a_own)

    @pl.when(b_even)
    def _():
        start(b_own)

    @pl.when(a_even)
    def _():
        a_arrived(0, other)
        start(a_swapped)

    @pl.when(jnp.logical_not(a_even))
    def _():
        forward(a_arrived, 1, mine, odd[0])

    @pl.when(b_even)
    def _():
        b_arrived(0, bother)
        start(b_swapped)

    @pl.when(jnp.logical_not(b_even))
    def _():
        forward(b_arrived, 1, bmine, b_far[0])

    @pl.when(a_even)
    def _():
        forward(a_arrived, 2, mine, even[0])

    @pl.when(jnp.logical_not(a_even))
    def _():
        forward(a_arrived, 1, other, odd[1])
        forward(a_arrived, 3, mine, odd_far[0])

    @pl.when(a_even)
    def _():
        forward(a_arrived, 2, other, even[1])

    @pl.when(jnp.logical_not(b_even))
    def _():
        forward(b_arrived, 1, bother, b_far[1])

    @pl.when(jnp.logical_not(a_even))
    def _():
        forward(a_arrived, 3, other, odd_far[1])

    @pl.when(a_even)
    def _():
        for sub in (mine, other):
            for part in range(2):
                a_arrived(4, sub, part)

    @pl.when(b_even)
    def _():
        for sub in (bmine, bother):
            for part in range(2):
                b_arrived(2, sub, part)

    def c_copy(m):
        rows = pl.ds(pl.multiple_of(m * LANES, LANES), LANES)
        return pltpu.make_async_remote_copy(
            src_ref=pbuf.at[rows, :], dst_ref=rbuf.at[rows, :],
            send_sem=csend.at[m], recv_sem=crecv.at[m],
            device_id=core_peer, device_id_type=MESH,
        )

    def one_row(m, carry):
        base = pl.multiple_of(m * BS, BS)
        column = lax.broadcasted_iota(jnp.int32, (COLS, LANES), 0)
        wanted = [ci_ref[m, t] for t in range(4)]
        total = jnp.zeros((BS, 4 * BS), jnp.float32)
        for zs in range(4):
            lhs = jnp.concatenate([abuf[zs, y, pl.ds(base, BS), :] for y in range(2)], axis=1)
            tags = [
                abuf[zs, y, pl.ds(A_DATA + m * 2 + s, 1), :] for y in range(2) for s in range(2)
            ]
            sides = []
            for p in range(2):
                got, ids = [], []
                for t in (2 * p, 2 * p + 1):
                    n = jnp.maximum(wanted[t], 0)
                    got.append(bbuf[zs // 2, zs % 2, pl.ds(n * 4, 4)].reshape(BS, LANES))
                    tag = jnp.where(column == wanted[t], bbuf[zs // 2, zs % 2, B_DATA], 0.0)
                    ids.append(jnp.sum(tag, axis=0, keepdims=True))
                straight = jnp.where(left, got[0], got[1])
                crossed = pltpu.roll(jnp.where(left, got[1], got[0]), BS, 1)
                tag_straight = jnp.where(left, ids[0], ids[1])
                tag_crossed = pltpu.roll(jnp.where(left, ids[1], ids[0]), BS, 1)
                sides.append(jnp.concatenate([
                    jnp.where(t == tag_straight, straight, jnp.where(t == tag_crossed, crossed, 0.0))
                    for t in tags
                ], axis=0))
            rhs = jnp.concatenate(sides, axis=1)
            l_hi = lhs.astype(jnp.bfloat16)
            l_lo = (lhs - l_hi.astype(jnp.float32)).astype(jnp.bfloat16)
            r_hi = rhs.astype(jnp.bfloat16)
            r_lo = (rhs - r_hi.astype(jnp.float32)).astype(jnp.bfloat16)
            for l, r in ((l_hi, r_lo), (l_lo, r_hi), (l_hi, r_hi)):
                total += jnp.dot(l, r, preferred_element_type=jnp.float32)
        out = pl.multiple_of(m * LANES, LANES)
        for p in range(2):
            v0 = total[:32, p * LANES : (p + 1) * LANES]
            v1 = total[32:, p * LANES : (p + 1) * LANES]
            low, high = halves(v0, v1, left)
            pbuf[pl.ds(out + 2 * p, 32, stride=4), :] = low
            pbuf[pl.ds(out + 2 * p + 1, 32, stride=4), :] = high
        c_copy(m).start()
        return carry

    lax.fori_loop(0, ROWS, one_row, 0)

    for m in range(ROWS):
        c_copy(m).wait_recv()
        rows = pl.ds(m * LANES, LANES)
        o_ref[rows, :] = pbuf[rows, :] + rbuf[rows, :]
    for m in range(ROWS):
        c_copy(m).wait_send()

    @pl.when(a_even)
    def _():
        for c in a_own + a_swapped + even[0] + even[1]:
            c.wait_send()

    @pl.when(jnp.logical_not(a_even))
    def _():
        for c in odd[0] + odd[1] + odd_far[0] + odd_far[1]:
            c.wait_send()

    @pl.when(b_even)
    def _():
        for c in b_own + b_swapped:
            c.wait_send()

    @pl.when(jnp.logical_not(b_even))
    def _():
        for c in b_far[0] + b_far[1]:
            c.wait_send()


def interleaved(blocks):
    r, s, _ = blocks.shape
    return blocks.reshape(r, s, 32, LANES).transpose(0, 2, 1, 3).reshape(r * 32 * s, LANES)


def per_device(a_blocks, a_index, b_blocks, b_index, c_index):
    vmem = pl.BlockSpec(memory_space=pltpu.VMEM)
    smem = pl.BlockSpec(memory_space=pltpu.SMEM)
    out = pl.pallas_call(
        kernel,
        out_shape=jax.ShapeDtypeStruct((ROWS * LANES, LANES), jnp.float32),
        in_specs=[vmem, smem, vmem, smem, smem],
        out_specs=vmem,
        scratch_shapes=[
            pltpu.VMEM((4, 2, A_CHUNK, LANES), jnp.float32),
            pltpu.VMEM((2, 2, B_CHUNK, COLS, LANES), jnp.float32),
            pltpu.VMEM((ROWS * LANES, LANES), jnp.float32),
            pltpu.VMEM((ROWS * LANES, LANES), jnp.float32),
            pltpu.SemaphoreType.DMA((9,)),
            pltpu.SemaphoreType.DMA((4, 2, 2)),
            pltpu.SemaphoreType.DMA((5,)),
            pltpu.SemaphoreType.DMA((2, 2, 2)),
            pltpu.SemaphoreType.DMA((ROWS,)),
            pltpu.SemaphoreType.DMA((ROWS,)),
        ],
        compiler_params=pltpu.CompilerParams(
            collective_id=0, has_side_effects=True, vmem_limit_bytes=32 << 20
        ),
    )(interleaved(a_blocks), a_index, interleaved(b_blocks), b_index, c_index)
    return out.reshape(ROWS, 32, 4, LANES).transpose(0, 2, 1, 3).reshape(ROWS, 4, BS * BS)


def solution(mesh):
    placed = (
        P("row", "col", None),
        P("row", "col"),
        P("col", "row", None),
        P("col", "row"),
        P("row", "col"),
    )
    return jax.shard_map(
        per_device, mesh=mesh, in_specs=placed, out_specs=P("row", "col", None), check_vma=False
    )
```

time: 217 us -> 54.6 us (0.25)
  the two profiles are of different devices: /device:TPU:1 before, /device:TPU:7 now
where the time goes in v1:
time: 54.6 us; the launch traced here: 54.4 us
  Pallas kernels  49.5 us (91%)
  local copies, waits for them, and re-layouts  4.91 us (9%)
    pallas_call x1, Pallas kernels, per_device(): pl.pallas_call(kernel, out_shape=jax.ShapeDtypeStruct((ROWS * LANES, LANE...  49.5 us
    unnamed x14, local copies, waits for them, and re-layouts  4.91 us

profile of v1, /device:TPU:7, one launch (start us, length us, event | category | flops | bytes accessed | tf_op | source)
XLA Modules:
  0.0 54.4 jit_solution(8091082923887373322)
XLA Ops:
  0.0 0.0 copy-start.3
  0.0 0.7 %copy-done.3 = s32[8,2]{0,1:T(2,128)S(1)} copy-done((s32[8,2]{0,1:T(2,128)S(1)}, s32[8,2]{0,1:T(2,128)}, u32[]{:S(2)}) %copy-start.3) | copy-done | bytes 88
  0.7 0.0 copy-start.2
  0.7 0.1 copy.8.ai_ref
  0.8 0.6 %copy-done.2 = s32[8,4]{0,1:T(4,128)S(1)} copy-done((s32[8,4]{0,1:T(4,128)S(1)}, s32[8,4]{0,1:T(4,128)}, u32[]{:S(2)}) %copy-start.2) | copy-done | bytes 152
  1.4 0.0 copy-start.4
  1.4 0.1 copy.10.ci_ref
  1.4 0.6 %copy-done.4 = s32[16,2]{0,1:T(2,128)S(1)} copy-done((s32[16,2]{0,1:T(2,128)S(1)}, s32[16,2]{0,1:T(2,128)}, u32[]{:S(2)}) %copy-start.4) | copy-done | bytes 152
  2.0 0.1 copy.9.bi_ref
  2.1 0.0 copy-start
  2.1 1.0 %copy-done = f32[16,2,4096]{2,1,0:T(2,128)S(1)} copy-done((f32[16,2,4096]{2,1,0:T(2,128)S(1)}, f32[16,2,4096]{2,1,0:T(2,128)}, u32[]{:S(2)}) %copy-start) | copy-done | bytes 524312
  3.2 0.0 copy-start.1
  3.2 0.9 %copy-done.1 = f32[8,2,4096]{2,1,0:T(2,128)S(1)} copy-done((f32[8,2,4096]{2,1,0:T(2,128)S(1)}, f32[8,2,4096]{2,1,0:T(2,128)}, u32[]{:S(2)}) %copy-start.1) | copy-done | bytes 262168
  4.1 49.5 %shard_map.55 = f32[1024,128]{1,0:T(8,128)S(1)} custom-call(f32[512,128]{1,0:T(8,128)S(1)} %bitcast.17, s32[8,2]{1,0:T(8,128)S(1)} %copy.8.ai_ref, f32[1024,128]{1,0:T(8,128)S(1)} %bitcast.16, s32[16,2]{1,0:T(8,128)S(1)} %copy.9.bi_ref, s32[8,4]{1,0:T(8,128)S(1)} %copy.10.ci_ref), custom_call_target="tpu_custom_call" | custom-call | tf_op jit(solution)/shard_map/pallas_call | solution.py:309
  53.6 0.8 %copy.13 = f32[8,4,4096]{2,1,0:T(4,128)} copy(f32[8,4,4096]{2,1,0:T(4,128)S(1)} %bitcast.15) | data formatting | bytes 1048576
Async XLA Ops:
  0.0 0.7 %copy-start.3 = (s32[8,2]{0,1:T(2,128)S(1)}, s32[8,2]{0,1:T(2,128)}, u32[]{:S(2)}) copy-start(s32[8,2]{0,1:T(2,128)} %param.6) | copy-start | bytes 196
  0.7 0.7 %copy-start.2 = (s32[8,4]{0,1:T(4,128)S(1)}, s32[8,4]{0,1:T(4,128)}, u32[]{:S(2)}) copy-start(s32[8,4]{0,1:T(4,128)} %param.9) | copy-start | bytes 388
  1.4 0.7 %copy-start.4 = (s32[16,2]{0,1:T(2,128)S(1)}, s32[16,2]{0,1:T(2,128)}, u32[]{:S(2)}) copy-start(s32[16,2]{0,1:T(2,128)} %param.8) | copy-start | bytes 388
  2.1 1.0 %copy-start = (f32[16,2,4096]{2,1,0:T(2,128)S(1)}, f32[16,2,4096]{2,1,0:T(2,128)}, u32[]{:S(2)}) copy-start(f32[16,2,4096]{2,1,0:T(2,128)} %param.7) | copy-start | bytes 1572868
  3.2 0.9 %copy-start.1 = (f32[8,2,4096]{2,1,0:T(2,128)S(1)}, f32[8,2,4096]{2,1,0:T(2,128)}, u32[]{:S(2)}) copy-start(f32[8,2,4096]{2,1,0:T(2,128)} %param.5) | copy-start | bytes 786436

commit v2 on v0

v2 whole, which is shorter than its diff:
```python
import jax
import jax.numpy as jnp
from jax import lax
from jax.experimental import pallas as pl
from jax.experimental.pallas import tpu as pltpu
from jax.sharding import PartitionSpec as P

BS = 64
LANES = 128
ROWS = 8
MINE = 4
COLS = 16
A_DATA = MINE * BS
A_PIECE = A_DATA + MINE * 2
GROUP = 16
B_HALF = COLS // 2 * 4 + 1
B_PARTS = ((0, 17), (17, 16))
TAGS = (0, 2 * B_HALF - 1)
X, Z = 4, 8
MESH = pl.DeviceIdType.MESH


def halves(x0, x1, left):
    return (
        jnp.where(left, x0, pltpu.roll(x1, BS, 1)),
        jnp.where(left, pltpu.roll(x0, BS, 1), x1),
    )


def kernel(
    a_hbm, ai_ref, b_hbm, bi_ref, ci_ref, o_ref,
    a_own, b_own, abuf, bbuf, total,
    isem, asend, arecv, bsend, brecv, fsend, frecv, csend, crecv,
):
    d = lax.axis_index("depth")
    row = lax.axis_index("row")
    col = lax.axis_index("col")
    x, yl = row % X, row // X
    z, yh = col // 2, col % 2
    way = 1 - 2 * d

    def z_at(k):
        return (z + Z - k * way) % Z

    def x_at(k):
        return (x + X - k * way) % X

    next_z = {"depth": d, "row": row, "col": z_at(-1) * 2 + yh}
    last_z = {"depth": d, "row": row, "col": z_at(1) * 2 + yh}
    next_x = {"depth": d, "row": yl * X + x_at(-1), "col": col}
    last_x = {"depth": d, "row": yl * X + x_at(1), "col": col}
    yh_peer = {"depth": d, "row": row, "col": z * 2 + (1 - yh)}
    yl_peer = {"depth": d, "row": (1 - yl) * X + x, "col": col}
    core_peer = {"depth": 1 - d, "row": row, "col": col}

    barrier = pltpu.get_barrier_semaphore()
    for peer in (next_z, last_z, next_x, last_x, yh_peer, yl_peer, core_peer):
        pl.semaphore_signal(barrier, inc=1, device_id=peer, device_id_type=MESH)

    mine_rows = pl.ds(pl.multiple_of(d * A_DATA, A_DATA), A_DATA)
    fetch_a = pltpu.make_async_copy(a_hbm.at[mine_rows, :], a_own, isem.at[0])
    fetch_b = pltpu.make_async_copy(b_hbm, b_own, isem.at[1])
    fetch_a.start()
    fetch_b.start()
    left = lax.broadcasted_iota(jnp.int32, (1, LANES), 1) < BS
    total[...] = jnp.zeros_like(total)

    fetch_a.wait()
    for m in range(MINE):
        x0 = a_own[pl.ds(m * BS, 32, stride=2), :]
        x1 = a_own[pl.ds(m * BS + 1, 32, stride=2), :]
        low, high = halves(x0, x1, left)
        abuf[z, yh, m * BS : m * BS + 32, :] = low
        abuf[z, yh, m * BS + 32 : m * BS + 64, :] = high
        for s in range(2):
            v = jnp.full((1, LANES), ai_ref[s, d * MINE + m])
            v = jnp.where(v < 0, -1, v + 1).astype(jnp.float32)
            r = A_DATA + m * 2 + s
            abuf[z, yh, r : r + 1, :] = v
    fetch_b.wait()
    for n in range(COLS):
        x0 = b_own[pl.ds(n * BS, 32, stride=2), :]
        x1 = b_own[pl.ds(n * BS + 1, 32, stride=2), :]
        low, high = halves(x0, x1, left)
        for g in range(4):
            group = 1 + n * 4 + g
            bbuf[row, group, pl.ds(0, 8, stride=2), :] = low[g * 8 : g * 8 + 8]
            bbuf[row, group, pl.ds(1, 8, stride=2), :] = high[g * 8 : g * 8 + 8]
        v0 = jnp.full((1, LANES), bi_ref[0, n])
        v1 = jnp.full((1, LANES), bi_ref[1, n])
        v = (jnp.where(left, v0, v1) + 1).astype(jnp.float32)
        r = n % 8
        bbuf[row, TAGS[n // 8], r : r + 1, :] = v

    pl.semaphore_wait(barrier, 7)

    a_y = (yh, 1 - yh)
    b_y = (yl, 1 - yl)

    def remote(view, to, send, recv):
        return pltpu.make_async_remote_copy(
            src_ref=view, dst_ref=view, send_sem=send, recv_sem=recv,
            device_id=to, device_id_type=MESH,
        )

    started = []

    def start(copy):
        copy.start()
        started.append(copy)

    def a_view(k, sub):
        return abuf.at[z_at(k), a_y[sub]]

    def b_view(k, sub, half, part):
        first, size = B_PARTS[part]
        return bbuf.at[b_y[sub] * X + x_at(k), pl.ds(half * B_HALF + first, size)]

    def a_next(k, sub):
        start(remote(a_view(k, sub), next_z, asend.at[k, sub], arecv.at[k + 1, sub]))

    def a_swap():
        start(remote(a_view(0, 0), yh_peer, asend.at[Z - 1, 0], arecv.at[0, 1]))

    def a_wait(k, sub):
        remote(a_view(k, sub), next_z, asend.at[0, 0], arecv.at[k, sub]).wait_recv()

    def b_next(k, sub, part):
        start(remote(b_view(k, sub, d, part), next_x, bsend.at[k, sub, part], brecv.at[k + 1, sub, part]))

    def b_swap(k, part):
        start(remote(b_view(k, 0, d, part), yl_peer, bsend.at[X + k, 0, part], brecv.at[k, 1, part]))

    def b_wait(k, sub, part):
        remote(b_view(k, sub, d, part), next_x, bsend.at[0, 0, 0], brecv.at[k, sub, part]).wait_recv()

    def b_share(k, sub, part):
        chunk = b_y[sub] * X + x_at(k)
        start(remote(b_view(k, sub, d, part), core_peer, fsend.at[chunk, part], frecv.at[chunk, part]))

    def b_shared(k, sub, part):
        chunk = b_y[sub] * X + x_at(k)
        view = b_view(k, sub, 1 - d, part)
        remote(view, core_peer, fsend.at[chunk, part], frecv.at[chunk, part]).wait_recv()

    def a_step(k, sub):
        a_wait(k, sub)
        a_next(k, sub)

    def b_step(k, sub, part):
        b_wait(k, sub, part)
        if (k, sub) in ((0, 1), (1, 0), (2, 0), (1, 1)):
            b_next(k, sub, part)
        if (k, sub) == (3, 0):
            b_swap(3, part)
        b_share(k, sub, part)

    column = lax.broadcasted_iota(jnp.int32, (8, LANES), 0)

    def tile(k, m):
        zs = z_at(k)
        base = m * BS
        if not isinstance(m, int):
            base = pl.multiple_of(base, BS)
        wanted = [ci_ref[t, d * MINE + m] for t in range(4)]
        lhs = jnp.concatenate([abuf[zs, y, pl.ds(base, BS), :] for y in range(2)], axis=1)
        tags = [abuf[zs, y, pl.ds(A_DATA + m * 2 + s, 1), :] for y in range(2) for s in range(2)]
        sides = []
        for p in range(2):
            got, ids = [], []
            for t in (2 * p, 2 * p + 1):
                n = jnp.maximum(wanted[t], 0)
                got.append(bbuf[zs, pl.ds(n * 4 + 1, 4)].reshape(BS, LANES))
                tag = jnp.where(column == wanted[t], bbuf[zs, TAGS[0], 0:8, :], 0.0)
                tag += jnp.where(column + 8 == wanted[t], bbuf[zs, TAGS[1], 0:8, :], 0.0)
                ids.append(jnp.sum(tag, axis=0, keepdims=True))
            straight = jnp.where(left, got[0], got[1])
            crossed = pltpu.roll(jnp.where(left, got[1], got[0]), BS, 1)
            tag_straight = jnp.where(left, ids[0], ids[1])
            tag_crossed = pltpu.roll(jnp.where(left, ids[1], ids[0]), BS, 1)
            sides.append(jnp.concatenate([
                jnp.where(t == tag_straight, straight, jnp.where(t == tag_crossed, crossed, 0.0))
                for t in tags
            ], axis=0))
        rhs = jnp.concatenate(sides, axis=1)
        l_hi = lhs.astype(jnp.bfloat16)
        l_lo = (lhs - l_hi.astype(jnp.float32)).astype(jnp.bfloat16)
        r_hi = rhs.astype(jnp.bfloat16)
        r_lo = (rhs - r_hi.astype(jnp.float32)).astype(jnp.bfloat16)
        new = total[m]
        for l, r in ((l_hi, r_lo), (l_lo, r_hi), (l_hi, r_hi)):
            new += jnp.dot(l, r, preferred_element_type=jnp.float32)
        return new

    def tiles(first, last):
        def body(i, carry):
            k, m = i // MINE, i % MINE
            total[m] = tile(k, m)
            return carry

        lax.fori_loop(first * MINE, last * MINE, body, 0)

    a_swap()
    a_next(0, 0)
    for part in range(2):
        b_next(0, 0, part)
    a_step(1, 0)
    b_step(1, 0, 0)
    a_step(0, 1)
    for part in range(2):
        b_swap(0, part)
    b_step(1, 0, 1)
    a_step(2, 0)
    b_step(2, 0, 0)
    a_step(1, 1)
    b_step(2, 0, 1)
    a_step(3, 0)
    b_step(3, 0, 0)
    a_step(2, 1)
    b_step(3, 0, 1)
    a_step(4, 0)
    b_step(0, 1, 0)
    a_step(3, 1)
    b_step(0, 1, 1)
    a_step(5, 0)
    b_step(1, 1, 0)
    a_step(4, 1)
    b_step(1, 1, 1)
    b_step(3, 1, 0)
    b_step(3, 1, 1)
    a_step(6, 0)
    b_step(2, 1, 0)
    a_step(5, 1)
    b_step(2, 1, 1)
    for k in range(X):
        for sub in range(2):
            if (k, sub) != (0, 0):
                for part in range(2):
                    b_shared(k, sub, part)
    tiles(0, 2)
    a_step(6, 1)
    tiles(2, 7)
    a_wait(7, 0)
    a_wait(7, 1)

    def c_copy(m):
        at = pl.ds(pl.multiple_of((d * MINE + m) * LANES, LANES), LANES)
        return remote(o_ref.at[at, :], core_peer, csend.at[m], crecv.at[m])

    def last(m, carry):
        done = tile(7, m)
        out = pl.multiple_of((d * MINE + m) * LANES, LANES)
        for p in range(2):
            v0 = done[:32, p * LANES : (p + 1) * LANES]
            v1 = done[32:, p * LANES : (p + 1) * LANES]
            low, high = halves(v0, v1, left)
            o_ref[pl.ds(out + 2 * p, 32, stride=4), :] = low
            o_ref[pl.ds(out + 2 * p + 1, 32, stride=4), :] = high
        c_copy(m).start()
        return carry

    lax.fori_loop(0, MINE, last, 0)

    for copy in started:
        copy.wait_send()
    for m in range(MINE):
        at = pl.ds(pl.multiple_of(((1 - d) * MINE + m) * LANES, LANES), LANES)
        remote(o_ref.at[at, :], core_peer, csend.at[m], crecv.at[m]).wait_recv()
        c_copy(m).wait_send()


def interleaved(blocks):
    r, s, _ = blocks.shape
    return blocks.reshape(r, s, 32, LANES).transpose(0, 2, 1, 3).reshape(r * 32 * s, LANES)


def per_device(a_blocks, a_index, b_blocks, b_index, c_index):
    vmem = pl.BlockSpec(memory_space=pltpu.VMEM)
    smem = pl.BlockSpec(memory_space=pltpu.SMEM)
    hbm = pl.BlockSpec(memory_space=pltpu.HBM)
    dma = pltpu.SemaphoreType.DMA
    out = pl.pallas_call(
        kernel,
        out_shape=jax.ShapeDtypeStruct((ROWS * LANES, LANES), jnp.float32),
        in_specs=[hbm, smem, hbm, smem, smem],
        out_specs=vmem,
        scratch_shapes=[
            pltpu.VMEM((A_DATA, LANES), jnp.float32),
            pltpu.VMEM((COLS * BS, LANES), jnp.float32),
            pltpu.VMEM((Z, 2, A_PIECE, LANES), jnp.float32),
            pltpu.VMEM((2 * X, 2 * B_HALF, GROUP, LANES), jnp.float32),
            pltpu.VMEM((MINE, BS, 4 * BS), jnp.float32),
            dma((2,)),
            dma((Z, 2)),
            dma((Z, 2)),
            dma((2 * X, 2, 2)),
            dma((X, 2, 2)),
            dma((2 * X, 2)),
            dma((2 * X, 2)),
            dma((MINE,)),
            dma((MINE,)),
        ],
        compiler_params=pltpu.CompilerParams(
            collective_id=0, has_side_effects=True, vmem_limit_bytes=56 << 20
        ),
    )(interleaved(a_blocks), a_index.T, interleaved(b_blocks), b_index.T, c_index.T)
    return out.reshape(ROWS, 32, 4, LANES).transpose(0, 2, 1, 3).reshape(ROWS, 4, BS * BS)


def solution(mesh):
    placed = (
        P("row", "col", None),
        P("row", "col"),
        P("col", "row", None),
        P("col", "row"),
        P("row", "col"),
    )
    return jax.shard_map(
        per_device, mesh=mesh, in_specs=placed, out_specs=P("row", "col", None), check_vma=False
    )
```

time: 217 us -> 53.4 us (0.25)
  local copies, waits for them, and re-layouts: 64.1 us -> 1.87 us
  blocking collectives: 60.1 us -> 0 us
  waiting for transfers between devices: 55.7 us -> 0 us
  Pallas kernels: 0 us -> 51.4 us
  matrix products: 20.6 us -> 0 us
  between operations: 13.5 us -> 0.01 us
    all_gather x3 -> x0, blocking collectives: 60.1 us -> none  [the longest x1 38.3 us: per_device(): a_ids = lax.all_gather(a_ids_send, 'col', axis=1, tiled=True)]
    all_gather x2 -> x0, waiting for transfers between devices: 55.7 us -> none  [the longest x1 55.6 us: per_device(): a_part = lax.all_gather(a_send, 'col', axis=1, tiled=True)]
    pallas_call x0 -> x1, Pallas kernels: none -> 51.4 us  [per_device(): pl.pallas_call(kernel, out_shape=jax.ShapeDtypeStruct((ROWS * LANES, LANE...]
    gather x4 -> x0, local copies, waits for them, and re-layouts: 35.7 us -> none  [the longest x2 31.1 us: per_device(): chosen = b_four[c_safe[:, :, None], jnp.where(usable, u_ids, 0)]]
    dot_general x1 -> x0, matrix products: 20.6 us -> none  [per_device(): jnp.einsum('rsac,rtscx->rtax', a_four, chosen, precision=lax.Precision.HI...]
    reshape x3 -> x0, local copies, waits for them, and re-layouts: 15.9 us -> none  [the longest x1 7.87 us: per_device(): b_four = b_whole.reshape(cols_dev, b_ids.shape[1], BS, BS)]
    all_gather x2 -> x0, local copies, waits for them, and re-layouts: 7.7 us -> none  [the longest x1 6.57 us: per_device(): a_part = lax.all_gather(a_send, 'col', axis=1, tiled=True)]
    unnamed x4 -> x1, local copies, waits for them, and re-layouts: 4.1 us -> 1.87 us
  transfers between devices with their start and end apart: 2 -> 0, of which waited for: 1 -> 0; matrix products, arithmetic and copies ran while one was open for 22% -> 0% of each run, Pallas kernels for 0% -> 0%
where the time goes in v2:
time: 53.4 us; the launch traced here: 53.2 us
  Pallas kernels  51.4 us (96%)
  local copies, waits for them, and re-layouts  1.87 us (4%)
    pallas_call x1, Pallas kernels, per_device(): pl.pallas_call(kernel, out_shape=jax.ShapeDtypeStruct((ROWS * LANES, LANE...  51.4 us
    unnamed x1, local copies, waits for them, and re-layouts  1.87 us

profile of v2, /device:TPU:1, one launch (start us, length us, event | category | flops | bytes accessed | tf_op | source)
XLA Modules:
  0.0 53.2 jit_solution(802623840784037441)
XLA Ops:
  0.0 51.4 %shard_map.55 = f32[1024,128]{1,0:T(8,128)} custom-call(f32[512,128]{1,0:T(8,128)} %bitcast.20, s32[2,8]{1,0:T(2,128)} %bitcast.22, f32[1024,128]{1,0:T(8,128)} %bitcast.19, s32[2,16]{1,0:T(2,128)} %bitcast.23, s32[4,8]{1,0:T(4,128)} %bitcast.21), custom_call_target="tpu_custom_call" | custom-call | tf_op jit(solution)/shard_map/pallas_call | solution.py:282
  51.4 1.9 %copy.10 = f32[8,4,4096]{2,1,0:T(4,128)} copy(f32[8,4,4096]{2,1,0:T(4,128)} %bitcast.18) | data formatting | bytes 1048576

commit v3 on v2

--- a/solution.py
+++ b/solution.py
@@ -15,8 +15,10 @@
 GROUP = 16
 B_HALF = COLS // 2 * 4 + 1
 B_PARTS = ((0, 17), (17, 16))
+A_PARTS = ((0, 136), (136, 128))
 TAGS = (0, 2 * B_HALF - 1)
 X, Z = 4, 8
+WAYS = (1, -1)
 MESH = pl.DeviceIdType.MESH
 
 
@@ -37,24 +39,21 @@
     col = lax.axis_index("col")
     x, yl = row % X, row // X
     z, yh = col // 2, col % 2
-    way = 1 - 2 * d
 
     def z_at(k):
-        return (z + Z - k * way) % Z
+        return (z + k + Z) % Z
 
     def x_at(k):
-        return (x + X - k * way) % X
-
-    next_z = {"depth": d, "row": row, "col": z_at(-1) * 2 + yh}
-    last_z = {"depth": d, "row": row, "col": z_at(1) * 2 + yh}
-    next_x = {"depth": d, "row": yl * X + x_at(-1), "col": col}
-    last_x = {"depth": d, "row": yl * X + x_at(1), "col": col}
+        return (x + k + X) % X
+
+    to_z = [{"depth": d, "row": row, "col": z_at(w) * 2 + yh} for w in WAYS]
+    to_x = [{"depth": d, "row": yl * X + x_at(w), "col": col} for w in WAYS]
     yh_peer = {"depth": d, "row": row, "col": z * 2 + (1 - yh)}
     yl_peer = {"depth": d, "row": (1 - yl) * X + x, "col": col}
     core_peer = {"depth": 1 - d, "row": row, "col": col}
 
     barrier = pltpu.get_barrier_semaphore()
-    for peer in (next_z, last_z, next_x, last_x, yh_peer, yl_peer, core_peer):
+    for peer in (*to_z, *to_x, yh_peer, yl_peer, core_peer):
         pl.semaphore_signal(barrier, inc=1, device_id=peer, device_id_type=MESH)
 
     mine_rows = pl.ds(pl.multiple_of(d * A_DATA, A_DATA), A_DATA)
@@ -109,59 +108,86 @@
         copy.start()
         started.append(copy)
 
-    def a_view(k, sub):
-        return abuf.at[z_at(k), a_y[sub]]
-
-    def b_view(k, sub, half, part):
+    def a_view(e, k, sub, part=None):
+        ref = abuf.at[z_at(-WAYS[e] * k), a_y[sub]]
+        return ref if part is None else ref.at[pl.ds(*A_PARTS[part]), :]
+
+    def a_next(e, k, sub, part=None):
+        view = a_view(e, k, sub, part)
+        start(remote(view, to_z[e], asend.at[e, k, sub], arecv.at[e, k + 1, sub]))
+
+    def a_swap():
+        start(remote(a_view(0, 0, 0), yh_peer, asend.at[0, 4, 0], arecv.at[0, 0, 1]))
+
+    def a_wait(e, k, sub, part=None):
+        remote(a_view(e, k, sub, part), to_z[e], asend.at[e, 0, 0], arecv.at[e, k, sub]).wait_recv()
+
+    def a_step(k, sub):
+        for e in range(2):
+            a_wait(e, k, sub)
+            a_next(e, k, sub, e if k == 3 else None)
+
+    def a_last(sub):
+        for e in range(2):
+            a_wait(e, 4, sub, e)
+
+    def a_other():
+        a_wait(0, 0, 1)
+        for e in range(2):
+            a_next(e, 0, 1)
+
+    def b_view(chunk, half, part):
         first, size = B_PARTS[part]
-        return bbuf.at[b_y[sub] * X + x_at(k), pl.ds(half * B_HALF + first, size)]
-
-    def a_next(k, sub):
-        start(remote(a_view(k, sub), next_z, asend.at[k, sub], arecv.at[k + 1, sub]))
-
-    def a_swap():
-        start(remote(a_view(0, 0), yh_peer, asend.at[Z - 1, 0], arecv.at[0, 1]))
-
-    def a_wait(k, sub):
-        remote(a_view(k, sub), next_z, asend.at[0, 0], arecv.at[k, sub]).wait_recv()
-
-    def b_next(k, sub, part):
-        start(remote(b_view(k, sub, d, part), next_x, bsend.at[k, sub, part], brecv.at[k + 1, sub, part]))
-
-    def b_swap(k, part):
-        start(remote(b_view(k, 0, d, part), yl_peer, bsend.at[X + k, 0, part], brecv.at[k, 1, part]))
-
-    def b_wait(k, sub, part):
-        remote(b_view(k, sub, d, part), next_x, bsend.at[0, 0, 0], brecv.at[k, sub, part]).wait_recv()
-
-    def b_share(k, sub, part):
-        chunk = b_y[sub] * X + x_at(k)
-        start(remote(b_view(k, sub, d, part), core_peer, fsend.at[chunk, part], frecv.at[chunk, part]))
-
-    def b_shared(k, sub, part):
-        chunk = b_y[sub] * X + x_at(k)
-        view = b_view(k, sub, 1 - d, part)
-        remote(view, core_peer, fsend.at[chunk, part], frecv.at[chunk, part]).wait_recv()
-
-    def a_step(k, sub):
-        a_wait(k, sub)
-        a_next(k, sub)
-
-    def b_step(k, sub, part):
-        b_wait(k, sub, part)
-        if (k, sub) in ((0, 1), (1, 0), (2, 0), (1, 1)):
-            b_next(k, sub, part)
-        if (k, sub) == (3, 0):
-            b_swap(3, part)
-        b_share(k, sub, part)
+        return bbuf.at[chunk, pl.ds(half * B_HALF + first, size)]
+
+    def b_chunk(e, k, sub):
+        return b_y[sub] * X + x_at(-WAYS[e] * k)
+
+    def b_next(e, k, sub, part):
+        view = b_view(b_chunk(e, k, sub), d, part)
+        start(remote(view, to_x[e], bsend.at[e, k, sub, part], brecv.at[e, k + 1, sub, part]))
+
+    def b_swap(part):
+        view = b_view(b_chunk(0, 0, 0), d, part)
+        start(remote(view, yl_peer, bsend.at[0, 2, 0, part], brecv.at[0, 0, 1, part]))
+
+    def b_take(e, k, sub, part):
+        chunk = b_chunk(e, k, sub)
+        view = b_view(chunk, d, part)
+        remote(view, to_x[e], bsend.at[e, 0, 0, part], brecv.at[e, k, sub, part]).wait_recv()
+        start(remote(view, core_peer, fsend.at[chunk, part], frecv.at[chunk, part]))
+
+    def b_step(sub):
+        for i in range(2):
+            for e in range(2):
+                part = e if i == 0 else 1 - e
+                b_take(e, 1, sub, part)
+                if i == 0:
+                    b_next(e, 1, sub, part)
+
+    def b_other(part):
+        b_take(0, 0, 1, part)
+        for e in range(2):
+            b_next(e, 0, 1, part)
+
+    def b_last(sub):
+        for e in range(2):
+            b_take(e, 2, sub, e)
+
+    def b_shared():
+        for k in range(X):
+            for sub in range(2):
+                if (k, sub) != (0, 0):
+                    chunk = b_chunk(0, k, sub)
+                    for part in range(2):
+                        view = b_view(chunk, 1 - d, part)
+                        remote(view, core_peer, fsend.at[chunk, part], frecv.at[chunk, part]).wait_recv()
 
     column = lax.broadcasted_iota(jnp.int32, (8, LANES), 0)
 
-    def tile(k, m):
+    def tile(new, k, m):
         zs = z_at(k)
-        base = m * BS
-        if not isinstance(m, int):
-            base = pl.multiple_of(base, BS)
+        base = pl.multiple_of(m * BS, BS)
         wanted = [ci_ref[t, d * MINE + m] for t in range(4)]
         lhs = jnp.concatenate([abuf[zs, y, pl.ds(base, BS), :] for y in range(2)], axis=1)
         tags = [abuf[zs, y, pl.ds(A_DATA + m * 2 + s, 1), :] for y in range(2) for s in range(2)]
@@ -187,68 +213,55 @@
         l_lo = (lhs - l_hi.astype(jnp.float32)).astype(jnp.bfloat16)
         r_hi = rhs.astype(jnp.bfloat16)
         r_lo = (rhs - r_hi.astype(jnp.float32)).astype(jnp.bfloat16)
-        new = total[m]
         for l, r in ((l_hi, r_lo), (l_lo, r_hi), (l_hi, r_hi)):
             new += jnp.dot(l, r, preferred_element_type=jnp.float32)
         return new
 
-    def tiles(first, last):
-        def body(i, carry):
-            k, m = i // MINE, i % MINE
-            total[m] = tile(k, m)
+    def summed(m, panels):
+        new = total[m]
+        for k in panels:
+            new = tile(new, k, m)
+        return new
+
+    def tiles(*panels):
+        def body(m, carry):
+            total[m] = summed(m, panels)
             return carry
 
-        lax.fori_loop(first * MINE, last * MINE, body, 0)
+        lax.fori_loop(0, MINE, body, 0)
 
     a_swap()
-    a_next(0, 0)
+    for e in range(2):
+        a_next(e, 0, 0)
+    for i in range(2):
+        for e in range(2):
+            b_next(e, 0, 0, e if i == 0 else 1 - e)
     for part in range(2):
-        b_next(0, 0, part)
+        b_swap(part)
     a_step(1, 0)
-    b_step(1, 0, 0)
-    a_step(0, 1)
-    for part in range(2):
-        b_swap(0, part)
-    b_step(1, 0, 1)
+    b_step(0)
+    a_other()
+    b_other(0)
     a_step(2, 0)
-    b_step(2, 0, 0)
+    b_other(1)
     a_step(1, 1)
-    b_step(2, 0, 1)
+    b_last(0)
     a_step(3, 0)
-    b_step(3, 0, 0)
     a_step(2, 1)
-    b_step(3, 0, 1)
-    a_step(4, 0)
-    b_step(0, 1, 0)
+    b_step(1)
+    a_last(0)
+    b_last(1)
     a_step(3, 1)
-    b_step(0, 1, 1)
-    a_step(5, 0)
-    b_step(1, 1, 0)
-    a_step(4, 1)
-    b_step(1, 1, 1)
-    b_step(3, 1, 0)
-    b_step(3, 1, 1)
-    a_step(6, 0)
-    b_step(2, 1, 0)
-    a_step(5, 1)
-    b_step(2, 1, 1)
-    for k in range(X):
-        for sub in range(2):
-            if (k, sub) != (0, 0):
-                for part in range(2):
-                    b_shared(k, sub, part)
-    tiles(0, 2)
-    a_step(6, 1)
-    tiles(2, 7)
-    a_wait(7, 0)
-    a_wait(7, 1)
+    b_shared()
+    tiles(0, 1, -1, 2, -2)
+    a_last(1)
 
     def c_copy(m):
         at = pl.ds(pl.multiple_of((d * MINE + m) * LANES, LANES), LANES)
         return remote(o_ref.at[at, :], core_peer, csend.at[m], crecv.at[m])
 
     def last(m, carry):
-        done = tile(7, m)
+        done = summed(m, (3, -3, 4))
         out = pl.multiple_of((d * MINE + m) * LANES, LANES)
         for p in range(2):
             v0 = done[:32, p * LANES : (p + 1) * LANES]
@@ -291,10 +304,10 @@
             pltpu.VMEM((2 * X, 2 * B_HALF, GROUP, LANES), jnp.float32),
             pltpu.VMEM((MINE, BS, 4 * BS), jnp.float32),
             dma((2,)),
-            dma((Z, 2)),
-            dma((Z, 2)),
-            dma((2 * X, 2, 2)),
-            dma((X, 2, 2)),
+            dma((2, 5, 2)),
+            dma((2, 5, 2)),
+            dma((2, 3, 2, 2)),
+            dma((2, 3, 2, 2)),
             dma((2 * X, 2)),
             dma((2 * X, 2)),
             dma((MINE,)),

time: 53.4 us -> 46.2 us (0.87)
  Pallas kernels: 51.4 us -> 44.2 us
    pallas_call x1, Pallas kernels: 51.4 us -> 44.2 us  [per_device(): pl.pallas_call(kernel, out_shape=jax.ShapeDtypeStruct((ROWS * LANES, LANE...]
where the time goes in v3:
time: 46.2 us; the launch traced here: 46.1 us
  Pallas kernels  44.2 us (96%)
  local copies, waits for them, and re-layouts  1.87 us (4%)
    pallas_call x1, Pallas kernels, per_device(): pl.pallas_call(kernel, out_shape=jax.ShapeDtypeStruct((ROWS * LANES, LANE...  44.2 us
    unnamed x1, local copies, waits for them, and re-layouts  1.87 us

profile of v3, /device:TPU:1, one launch (start us, length us, event | category | flops | bytes accessed | tf_op | source)
XLA Modules:
  0.0 46.1 jit_solution(14490404869754829999)
XLA Ops:
  0.0 44.2 %shard_map.55 = f32[1024,128]{1,0:T(8,128)} custom-call(f32[512,128]{1,0:T(8,128)} %bitcast.20, s32[2,8]{1,0:T(2,128)} %bitcast.22, f32[1024,128]{1,0:T(8,128)} %bitcast.19, s32[2,16]{1,0:T(2,128)} %bitcast.23, s32[4,8]{1,0:T(4,128)} %bitcast.21), custom_call_target="tpu_custom_call" | custom-call | tf_op jit(solution)/shard_map/pallas_call | solution.py:295
  44.2 1.9 %copy.10 = f32[8,4,4096]{2,1,0:T(4,128)} copy(f32[8,4,4096]{2,1,0:T(4,128)} %bitcast.18) | data formatting | bytes 1048576

commit v4 on v3

--- a/solution.py
+++ b/solution.py
@@ -30,8 +30,8 @@
 
 
 def kernel(
-    a_hbm, ai_ref, b_hbm, bi_ref, ci_ref, o_ref,
-    a_own, b_own, abuf, bbuf, total,
+    a_hbm, ai_hbm, b_hbm, bi_hbm, ci_hbm, o_ref,
+    ai_ref, bi_ref, ci_ref, a_own, b_own, abuf, bbuf, total,
     isem, asend, arecv, bsend, brecv, fsend, frecv, csend, crecv,
 ):
     d = lax.axis_index("depth")
@@ -48,6 +48,7 @@
 
     to_z = [{"depth": d, "row": row, "col": z_at(w) * 2 + yh} for w in WAYS]
     to_x = [{"depth": d, "row": yl * X + x_at(w), "col": col} for w in WAYS]
+    to_zy = [{"depth": d, "row": row, "col": z_at(w) * 2 + (1 - yh)} for w in WAYS]
     yh_peer = {"depth": d, "row": row, "col": z * 2 + (1 - yh)}
     yl_peer = {"depth": d, "row": (1 - yl) * X + x, "col": col}
     core_peer = {"depth": 1 - d, "row": row, "col": col}
@@ -60,11 +61,18 @@
     fetch_a = pltpu.make_async_copy(a_hbm.at[mine_rows, :], a_own, isem.at[0])
     fetch_b = pltpu.make_async_copy(b_hbm, b_own, isem.at[1])
     fetch_a.start()
+    fetch_ai = pltpu.make_async_copy(ai_hbm, ai_ref, isem.at[2])
+    fetch_bi = pltpu.make_async_copy(bi_hbm, bi_ref, isem.at[3])
+    fetch_ci = pltpu.make_async_copy(ci_hbm, ci_ref, isem.at[4])
+    fetch_ai.start()
     fetch_b.start()
+    fetch_bi.start()
+    fetch_ci.start()
     left = lax.broadcasted_iota(jnp.int32, (1, LANES), 1) < BS
     total[...] = jnp.zeros_like(total)
 
     fetch_a.wait()
+    fetch_ai.wait()
     for m in range(MINE):
         x0 = a_own[pl.ds(m * BS, 32, stride=2), :]
         x1 = a_own[pl.ds(m * BS + 1, 32, stride=2), :]
@@ -76,21 +84,6 @@
             v = jnp.where(v < 0, -1, v + 1).astype(jnp.float32)
             r = A_DATA + m * 2 + s
             abuf[z, yh, r : r + 1, :] = v
-    fetch_b.wait()
-    for n in range(COLS):
-        x0 = b_own[pl.ds(n * BS, 32, stride=2), :]
-        x1 = b_own[pl.ds(n * BS + 1, 32, stride=2), :]
-        low, high = halves(x0, x1, left)
-        for g in range(4):
-            group = 1 + n * 4 + g
-            bbuf[row, group, pl.ds(0, 8, stride=2), :] = low[g * 8 : g * 8 + 8]
-            bbuf[row, group, pl.ds(1, 8, stride=2), :] = high[g * 8 : g * 8 + 8]
-        v0 = jnp.full((1, LANES), bi_ref[0, n])
-        v1 = jnp.full((1, LANES), bi_ref[1, n])
-        v = (jnp.where(left, v0, v1) + 1).astype(jnp.float32)
-        r = n % 8
-        bbuf[row, TAGS[n // 8], r : r + 1, :] = v
-
     pl.semaphore_wait(barrier, 7)
 
     a_y = (yh, 1 - yh)
@@ -108,33 +101,53 @@
         copy.start()
         started.append(copy)
 
-    def a_view(e, k, sub, part=None):
-        ref = abuf.at[z_at(-WAYS[e] * k), a_y[sub]]
-        return ref if part is None else ref.at[pl.ds(*A_PARTS[part]), :]
-
-    def a_next(e, k, sub, part=None):
+    def a_view(e, k, sub, part):
+        return abuf.at[z_at(-WAYS[e] * k), a_y[sub], pl.ds(*A_PARTS[part]), :]
+
+    def a_next(e, k, sub, part):
         view = a_view(e, k, sub, part)
-        start(remote(view, to_z[e], asend.at[e, k, sub], arecv.at[e, k + 1, sub]))
-
-    def a_swap():
-        start(remote(a_view(0, 0, 0), yh_peer, asend.at[0, 4, 0], arecv.at[0, 0, 1]))
-
-    def a_wait(e, k, sub, part=None):
-        remote(a_view(e, k, sub, part), to_z[e], asend.at[e, 0, 0], arecv.at[e, k, sub]).wait_recv()
-
-    def a_step(k, sub):
-        for e in range(2):
-            a_wait(e, k, sub)
-            a_next(e, k, sub, e if k == 3 else None)
+        start(remote(view, to_z[e], asend.at[e, k, sub, part], arecv.at[e, k + 1, sub, part]))
+
+    def a_swap(part):
+        view = a_view(0, 0, 0, part)
+        start(remote(view, yh_peer, asend.at[0, 4, 0, part], arecv.at[0, 0, 1, part]))
+
+    def a_across(e, part):
+        view = a_view(0, 0, 0, part)
+        start(remote(view, to_zy[e], asend.at[e, 0, 1, part], arecv.at[e, 1, 1, part]))
+
+    def a_wait(e, k, sub, part):
+        view = a_view(e, k, sub, part)
+        remote(view, to_z[e], asend.at[e, 0, 0, 0], arecv.at[e, k, sub, part]).wait_recv()
+
+    def a_over(e, k, part):
+        view = a_view(e, k, 0, part)
+        start(remote(view, yh_peer, asend.at[e, k, 1, part], arecv.at[e, k, 1, part]))
+
+    def a_step(k, sub, i):
+        for e in range(2):
+            part = i if sub else (e + i) % 2
+            a_wait(e, k, sub, part)
+            if k + sub < 3 or (k == 3 and part == e):
+                a_next(e, k, sub, part)
+            if k == 3:
+                a_over(e, k, part)
+
+    def a_other(part):
+        a_wait(0, 0, 1, part)
+        for e in range(2):
+            a_next(e, 0, 1, part)
 
     def a_last(sub):
         for e in range(2):
             a_wait(e, 4, sub, e)
-
-    def a_other():
-        a_wait(0, 0, 1)
-        for e in range(2):
-            a_next(e, 0, 1)
+            if sub == 0:
+                a_over(e, 4, e)
+
+    def a_far(k):
+        for e in range(2):
+            for part in range(2):
+                a_wait(e, k, 1, part)
 
     def b_view(chunk, half, part):
         first, size = B_PARTS[part]
@@ -157,13 +170,12 @@
         remote(view, to_x[e], bsend.at[e, 0, 0, part], brecv.at[e, k, sub, part]).wait_recv()
         start(remote(view, core_peer, fsend.at[chunk, part], frecv.at[chunk, part]))
 
-    def b_step(sub):
-        for i in range(2):
-            for e in range(2):
-                part = e if i == 0 else 1 - e
-                b_take(e, 1, sub, part)
-                if i == 0:
-                    b_next(e, 1, sub, part)
+    def b_step(sub, i):
+        for e in range(2):
+            part = i if sub else (e + i) % 2
+            b_take(e, 1, sub, part)
+            if part == e:
+                b_next(e, 1, sub, part)
 
     def b_other(part):
         b_take(0, 0, 1, part)
@@ -230,30 +242,56 @@
 
         lax.fori_loop(0, MINE, body, 0)
 
-    a_swap()
-    for e in range(2):
-        a_next(e, 0, 0)
+    a_swap(0)
     for i in range(2):
         for e in range(2):
-            b_next(e, 0, 0, e if i == 0 else 1 - e)
-    for part in range(2):
-        b_swap(part)
-    a_step(1, 0)
-    b_step(0)
-    a_other()
+            a_next(e, 0, 0, (e + i) % 2)
+    fetch_b.wait()
+    fetch_bi.wait()
+    fetch_ci.wait()
+    for n in range(COLS):
+        x0 = b_own[pl.ds(n * BS, 32, stride=2), :]
+        x1 = b_own[pl.ds(n * BS + 1, 32, stride=2), :]
+        low, high = halves(x0, x1, left)
+        for g in range(4):
+            group = 1 + n * 4 + g
+            bbuf[row, group, pl.ds(0, 8, stride=2), :] = low[g * 8 : g * 8 + 8]
+            bbuf[row, group, pl.ds(1, 8, stride=2), :] = high[g * 8 : g * 8 + 8]
+        v0 = jnp.full((1, LANES), bi_ref[0, n])
+        v1 = jnp.full((1, LANES), bi_ref[1, n])
+        v = (jnp.where(left, v0, v1) + 1).astype(jnp.float32)
+        r = n % 8
+        bbuf[row, TAGS[n // 8], r : r + 1, :] = v
+
+    b_swap(0)
+    a_swap(1)
+    b_swap(1)
+    for i in range(2):
+        for e in range(2):
+            b_next(e, 0, 0, (e + i) % 2)
+    a_step(1, 0, 0)
+    a_other(0)
+    a_step(1, 0, 1)
+    b_step(0, 0)
     b_other(0)
-    a_step(2, 0)
+    a_step(2, 0, 0)
+    b_step(0, 1)
+    a_other(1)
     b_other(1)
-    a_step(1, 1)
+    a_step(2, 0, 1)
+    a_step(1, 1, 0)
     b_last(0)
-    a_step(3, 0)
-    a_step(2, 1)
-    b_step(1)
+    a_step(3, 0, 0)
+    a_step(1, 1, 1)
+    a_step(3, 0, 1)
+    b_step(1, 0)
+    b_step(1, 1)
     a_last(0)
     b_last(1)
-    a_step(3, 1)
+    a_far(2)
     b_shared()
     tiles(0, 1, -1, 2, -2)
+    a_far(3)
     a_last(1)
 
     def c_copy(m):
@@ -289,23 +327,25 @@
 
 def per_device(a_blocks, a_index, b_blocks, b_index, c_index):
     vmem = pl.BlockSpec(memory_space=pltpu.VMEM)
-    smem = pl.BlockSpec(memory_space=pltpu.SMEM)
     hbm = pl.BlockSpec(memory_space=pltpu.HBM)
     dma = pltpu.SemaphoreType.DMA
     out = pl.pallas_call(
         kernel,
-        out_shape=jax.ShapeDtypeStruct((ROWS * LANES, LANES), jnp.float32),
-        in_specs=[hbm, smem, hbm, smem, smem],
+        out_shape=pltpu.VMEM((ROWS * LANES, LANES), jnp.float32),
+        in_specs=[hbm] * 5,
         out_specs=vmem,
         scratch_shapes=[
+            pltpu.SMEM((2, ROWS), jnp.int32),
+            pltpu.SMEM((2, COLS), jnp.int32),
+            pltpu.SMEM((4, ROWS), jnp.int32),
             pltpu.VMEM((A_DATA, LANES), jnp.float32),
             pltpu.VMEM((COLS * BS, LANES), jnp.float32),
             pltpu.VMEM((Z, 2, A_PIECE, LANES), jnp.float32),
             pltpu.VMEM((2 * X, 2 * B_HALF, GROUP, LANES), jnp.float32),
             pltpu.VMEM((MINE, BS, 4 * BS), jnp.float32),
-            dma((2,)),
-            dma((2, 5, 2)),
-            dma((2, 5, 2)),
+            dma((5,)),
+            dma((2, 5, 2, 2)),
+            dma((2, 5, 2, 2)),
             dma((2, 3, 2, 2)),
             dma((2, 3, 2, 2)),
             dma((2 * X, 2)),

time: 46.2 us -> 38.6 us (0.84)
  Pallas kernels: 44.2 us -> 37.8 us
  local copies, waits for them, and re-layouts: 1.87 us -> 0.8 us
    pallas_call x1, Pallas kernels: 44.2 us -> 37.8 us  [per_device(): pl.pallas_call(kernel, out_shape=pltpu.VMEM((ROWS * LANES, LANES), jnp.fl...]
    unnamed x1, local copies, waits for them, and re-layouts: 1.87 us -> 0.8 us
where the time goes in v4:
time: 38.6 us
  Pallas kernels  37.8 us (98%)
  local copies, waits for them, and re-layouts  0.8 us (2%)
    pallas_call x1, Pallas kernels, per_device(): pl.pallas_call(kernel, out_shape=pltpu.VMEM((ROWS * LANES, LANES), jnp.fl...  37.8 us
    unnamed x1, local copies, waits for them, and re-layouts  0.8 us

profile of v4, /device:TPU:1, one launch (start us, length us, event | category | flops | bytes accessed | tf_op | source)
XLA Modules:
  0.0 38.6 jit_solution(7283180305708804521)
XLA Ops:
  0.0 37.8 %shard_map.55 = f32[1024,128]{1,0:T(8,128)S(1)} custom-call(f32[512,128]{1,0:T(8,128)} %bitcast.20, s32[2,8]{1,0:T(2,128)} %bitcast.22, f32[1024,128]{1,0:T(8,128)} %bitcast.19, s32[2,16]{1,0:T(2,128)} %bitcast.23, s32[4,8]{1,0:T(4,128)} %bitcast.21), custom_call_target="tpu_custom_call" | custom-call | tf_op jit(solution)/shard_map/pallas_call | solution.py:332
  37.8 0.8 %copy.10 = f32[8,4,4096]{2,1,0:T(4,128)} copy(f32[8,4,4096]{2,1,0:T(4,128)S(1)} %bitcast.18) | data formatting | bytes 1048576

commit v5 on v4

--- a/solution.py
+++ b/solution.py
@@ -12,9 +12,9 @@
 COLS = 16
 A_DATA = MINE * BS
 A_PIECE = A_DATA + MINE * 2
-GROUP = 16
-B_HALF = COLS // 2 * 4 + 1
-B_PARTS = ((0, 17), (17, 16))
+GROUP = 8
+B_HALF = COLS // 2 * 8 + 1
+B_PARTS = ((0, 33), (33, 32))
 A_PARTS = ((0, 136), (136, 128))
 TAGS = (0, 2 * B_HALF - 1)
 X, Z = 4, 8
@@ -128,10 +128,8 @@
         for e in range(2):
             part = i if sub else (e + i) % 2
             a_wait(e, k, sub, part)
-            if k + sub < 3 or (k == 3 and part == e):
+            if k < 3 or (k == 3 and part == e):
                 a_next(e, k, sub, part)
-            if k == 3:
-                a_over(e, k, part)
 
     def a_other(part):
         a_wait(0, 0, 1, part)
@@ -174,7 +172,7 @@
         for e in range(2):
             part = i if sub else (e + i) % 2
             b_take(e, 1, sub, part)
-            if part == e:
+            if part == e and sub == 0:
                 b_next(e, 1, sub, part)
 
     def b_other(part):
@@ -182,9 +180,15 @@
         for e in range(2):
             b_next(e, 0, 1, part)
 
+    def b_over(e):
+        view = b_view(b_chunk(e, 2, 0), d, e)
+        start(remote(view, yl_peer, bsend.at[e, 2, 1, e], brecv.at[e, 2, 1, e]))
+
     def b_last(sub):
         for e in range(2):
             b_take(e, 2, sub, e)
+            if sub == 0:
+                b_over(e)
 
     def b_shared():
         for k in range(X):
@@ -196,6 +200,14 @@
                         remote(view, core_peer, fsend.at[chunk, part], frecv.at[chunk, part]).wait_recv()
 
     column = lax.broadcasted_iota(jnp.int32, (8, LANES), 0)
+
+    def split(value):
+        high = value.astype(jnp.bfloat16)
+        return high, (value - high.astype(jnp.float32)).astype(jnp.bfloat16)
+
+    def wide(mask):
+        row = jnp.where(mask, 1.0, 0.0)
+        return jnp.broadcast_to(row, (BS, LANES)).astype(jnp.bfloat16) > 0
 
     def tile(new, k, m):
         zs = z_at(k)
@@ -208,7 +220,7 @@
             got, ids = [], []
             for t in (2 * p, 2 * p + 1):
                 n = jnp.maximum(wanted[t], 0)
-                got.append(bbuf[zs, pl.ds(n * 4 + 1, 4)].reshape(BS, LANES))
+                got.append(bbuf[zs, pl.ds(n * 8 + 1, 8)].reshape(BS, LANES))
                 tag = jnp.where(column == wanted[t], bbuf[zs, TAGS[0], 0:8, :], 0.0)
                 tag += jnp.where(column + 8 == wanted[t], bbuf[zs, TAGS[1], 0:8, :], 0.0)
                 ids.append(jnp.sum(tag, axis=0, keepdims=True))
@@ -216,18 +228,22 @@
             crossed = pltpu.roll(jnp.where(left, got[1], got[0]), BS, 1)
             tag_straight = jnp.where(left, ids[0], ids[1])
             tag_crossed = pltpu.roll(jnp.where(left, ids[1], ids[0]), BS, 1)
-            sides.append(jnp.concatenate([
-                jnp.where(t == tag_straight, straight, jnp.where(t == tag_crossed, crossed, 0.0))
-                for t in tags
-            ], axis=0))
-        rhs = jnp.concatenate(sides, axis=1)
-        l_hi = lhs.astype(jnp.bfloat16)
-        l_lo = (lhs - l_hi.astype(jnp.float32)).astype(jnp.bfloat16)
-        r_hi = rhs.astype(jnp.bfloat16)
-        r_lo = (rhs - r_hi.astype(jnp.float32)).astype(jnp.bfloat16)
-        for l, r in ((l_hi, r_lo), (l_lo, r_hi), (l_hi, r_hi)):
-            new += jnp.dot(l, r, preferred_element_type=jnp.float32)
-        return new
+            straight, crossed = split(straight), split(crossed)
+            masks = [(wide(t == tag_straight), wide(t == tag_crossed)) for t in tags]
+            zero = jnp.zeros((BS, LANES), jnp.bfloat16)
+            sides.append([
+                jnp.concatenate([
+                    jnp.where(here, straight[i], jnp.where(there, crossed[i], zero))
+                    for here, there in masks
+                ], axis=0)
+                for i in range(2)
+            ])
+        r_hi, r_lo = (jnp.concatenate([side[i] for side in sides], axis=1) for i in range(2))
+        l_hi, l_lo = split(lhs)
+        low = jnp.dot(l_hi, r_lo, preferred_element_type=jnp.float32)
+        both = jnp.concatenate([l_hi, l_lo], axis=0)
+        both = jnp.dot(both, r_hi, preferred_element_type=jnp.float32)
+        return new + ((low + both[BS:]) + both[:BS])
 
     def summed(m, panels):
         new = total[m]
@@ -253,10 +269,10 @@
         x0 = b_own[pl.ds(n * BS, 32, stride=2), :]
         x1 = b_own[pl.ds(n * BS + 1, 32, stride=2), :]
         low, high = halves(x0, x1, left)
-        for g in range(4):
-            group = 1 + n * 4 + g
-            bbuf[row, group, pl.ds(0, 8, stride=2), :] = low[g * 8 : g * 8 + 8]
-            bbuf[row, group, pl.ds(1, 8, stride=2), :] = high[g * 8 : g * 8 + 8]
+        for g in range(8):
+            group = 1 + n * 8 + g
+            bbuf[row, group, pl.ds(0, 4, stride=2), :] = low[g * 4 : g * 4 + 4]
+            bbuf[row, group, pl.ds(1, 4, stride=2), :] = high[g * 4 : g * 4 + 4]
         v0 = jnp.full((1, LANES), bi_ref[0, n])
         v1 = jnp.full((1, LANES), bi_ref[1, n])
         v = (jnp.where(left, v0, v1) + 1).astype(jnp.float32)
@@ -283,12 +299,13 @@
     b_last(0)
     a_step(3, 0, 0)
     a_step(1, 1, 1)
+    b_step(1, 0)
     a_step(3, 0, 1)
-    b_step(1, 0)
     b_step(1, 1)
+    a_step(2, 1, 0)
     a_last(0)
     b_last(1)
-    a_far(2)
+    a_step(2, 1, 1)
     b_shared()
     tiles(0, 1, -1, 2, -2)
     a_far(3)

time: 38.6 us -> 37.2 us (0.964)
  Pallas kernels: 37.8 us -> 36.4 us
    pallas_call x1, Pallas kernels: 37.8 us -> 36.4 us  [per_device(): pl.pallas_call(kernel, out_shape=pltpu.VMEM((ROWS * LANES, LANES), jnp.fl...]
where the time goes in v5:
time: 37.2 us
  Pallas kernels  36.4 us (98%)
  local copies, waits for them, and re-layouts  0.8 us (2%)
    pallas_call x1, Pallas kernels, per_device(): pl.pallas_call(kernel, out_shape=pltpu.VMEM((ROWS * LANES, LANES), jnp.fl...  36.4 us
    unnamed x1, local copies, waits for them, and re-layouts  0.8 us

profile of v5, /device:TPU:1, one launch (start us, length us, event | category | flops | bytes accessed | tf_op | source)
XLA Modules:
  0.0 37.2 jit_solution(5723459194685385065)
XLA Ops:
  0.0 36.4 %shard_map.55 = f32[1024,128]{1,0:T(8,128)S(1)} custom-call(f32[512,128]{1,0:T(8,128)} %bitcast.20, s32[2,8]{1,0:T(2,128)} %bitcast.22, f32[1024,128]{1,0:T(8,128)} %bitcast.19, s32[2,16]{1,0:T(2,128)} %bitcast.23, s32[4,8]{1,0:T(4,128)} %bitcast.21), custom_call_target="tpu_custom_call" | custom-call | tf_op jit(solution)/shard_map/pallas_call | solution.py:349
  36.4 0.8 %copy.10 = f32[8,4,4096]{2,1,0:T(4,128)} copy(f32[8,4,4096]{2,1,0:T(4,128)S(1)} %bitcast.18) | data formatting | bytes 1048576
